TPU v7x, 256 devices: a whole 4x4x8 slice. The times are simulated.
256 devices in a mesh: layer: 16 (over z, core), sample: 16 (over y, x).
Axes of the slice: x: 4, y: 4, z: 8, core: 2. Of those that a mesh axis runs over, the one named last changes fastest.
Arguments:
- section_lengths: int32 [16], P('layer'), may hold values from 1 to 4, 40 in all
- forward_states: bfloat16 [16, 16, 32, 32, 128], P('layer', 'sample'), may hold values from -6 to 6
- adjoint_states: bfloat16 [16, 16, 32, 32, 128], P('layer', 'sample'), may hold values from -6 to 6
- weights: bfloat16 [64, 9, 128, 128], P('layer'), may hold values from -0.1875 to 0.1875
- biases: float32 [64, 128], P('layer'), may hold values from -3 to 3
Outputs:
- section_ends: bfloat16 [16, 16, 32, 32, 128], P('layer', 'sample')
- section_starts: bfloat16 [16, 16, 32, 32, 128], P('layer', 'sample')
- weight_grad: float32 [64, 9, 128, 128], P('layer', None, 'sample')
- bias_grad: float32 [64, 128], P('layer', 'sample')
Inputs may be any that keep to these rules, and one draw needn't show every extreme that they name: `section_lengths`: the lengths sum to 40, and some section holds exactly 4 layers.
All inputs are finite; a program needn't handle non-finite values. No bound on the sum of `section_lengths` on one device may be relied on, other than what follows from the above.
Results may differ from a plain program's by a relative error of at most 0.02.
Values may be sent and summed in bfloat16 or wider, within the bound.
No kernel may reach another device: no remote copies, remote signals or barrier semaphores. Data moves between devices by JAX's collectives and lax.ppermute only.
A program may use at most 64 MiB of HBM per device.

v0:
```python
import math

import jax
import jax.numpy as jnp
from jax import lax
from jax.sharding import PartitionSpec as P

STEP_SIZE = 0.5


def from_behind(block, axis, distance):
    devices = range(lax.axis_size(axis))
    route = [(i - distance, i) for i in devices if i - distance in devices]
    return lax.ppermute(block, axis, route)


def patches(inputs):
    height, width, channels = (inputs.shape[1], inputs.shape[2], inputs.shape[3])
    padded = jnp.pad(inputs, ((0, 0), (1, 1), (1, 1), (0, 0)))
    windows = [
        padded[:, row_off : row_off + height, col_off : col_off + width, :]
        for row_off in range(3)
        for col_off in range(3)
    ]
    return jnp.concatenate(windows, axis=-1).reshape(-1, 9 * channels)


def run_section(initial, weights, biases, length):
    channels = weights.shape[-1]
    current = initial
    patch_list = []
    tanh_list = []
    for layer_pos in range(weights.shape[0]):
        windows = patches(current.astype(jnp.bfloat16))
        summed = jnp.dot(
            windows,
            weights[layer_pos].reshape(9 * channels, channels),
            preferred_element_type=jnp.float32,
        )
        activity = jnp.tanh(summed + biases[layer_pos])
        advanced = current + STEP_SIZE * activity.reshape(current.shape)
        current = jnp.where(layer_pos < length, advanced, current)
        patch_list.append(windows)
        tanh_list.append(activity)
    return (current, patch_list, tanh_list)


def back_section(terminal, weights, patch_list, tanh_list, length, want_grads):
    channels = weights.shape[-1]
    adjoint = terminal
    count = weights.shape[0]
    weight_terms = [None] * count
    bias_terms = [None] * count
    for layer_pos in reversed(range(count)):
        signal = (
            STEP_SIZE * adjoint.reshape(-1, channels) * (1.0 - tanh_list[layer_pos] ** 2)
        ).astype(jnp.bfloat16)
        signal = jnp.where(layer_pos < length, signal, jnp.zeros_like(signal))
        flipped = jnp.swapaxes(weights[layer_pos][::-1], 1, 2).reshape(9 * channels, channels)
        back_term = jnp.dot(
            patches(signal.reshape(adjoint.shape)), flipped, preferred_element_type=jnp.float32
        )
        adjoint = adjoint + back_term.reshape(adjoint.shape)
        if want_grads:
            weight_terms[layer_pos] = lax.dot_general(
                patch_list[layer_pos],
                signal,
                (((0,), (0,)), ((), ())),
                preferred_element_type=jnp.float32,
            ).reshape(9, channels, channels)
            bias_terms[layer_pos] = jnp.sum(signal.astype(jnp.float32), axis=0)
    if want_grads:
        return (adjoint, jnp.stack(weight_terms), jnp.stack(bias_terms))
    return (adjoint, None, None)


def body(section_lengths, forward_states, adjoint_states, weights, biases):
    length = section_lengths[0]
    given_state = forward_states[0]
    given_adjoint = adjoint_states[0]
    propagated = run_section(given_state.astype(jnp.float32), weights, biases, length)[0]
    received = from_behind(propagated.astype(jnp.bfloat16), "layer", 1)
    leading = lax.axis_index("layer") == 0
    relaxed_state = jnp.where(leading, given_state, received)
    ending, patch_list, tanh_list = run_section(
        relaxed_state.astype(jnp.float32), weights, biases, length
    )
    back_start = back_section(
        given_adjoint.astype(jnp.float32), weights, patch_list, tanh_list, length, False
    )[0]
    received_back = from_behind(back_start.astype(jnp.bfloat16), "layer", -1)
    trailing = lax.axis_index("layer") == lax.axis_size("layer") - 1
    relaxed_adjoint = jnp.where(trailing, given_adjoint, received_back)
    adjoint, weight_terms, bias_terms = back_section(
        relaxed_adjoint.astype(jnp.float32), weights, patch_list, tanh_list, length, True
    )
    total_samples = forward_states.shape[1] * lax.axis_size("sample")
    factor = 1.0 / math.sqrt(total_samples * forward_states.shape[2] * forward_states.shape[3])
    weight_total, bias_total = (
        lax.psum(weight_terms.astype(jnp.bfloat16), "sample").astype(jnp.float32),
        lax.psum(bias_terms.astype(jnp.bfloat16), "sample").astype(jnp.float32),
    )
    share_rows = weight_terms.shape[2] // lax.axis_size("sample")
    offset = lax.axis_index("sample") * share_rows
    weight_part = lax.dynamic_slice_in_dim(weight_total, offset, share_rows, 2)
    bias_part = lax.dynamic_slice_in_dim(bias_total, offset, share_rows, 1)
    section_ends = ending.astype(jnp.bfloat16)[None]
    section_starts = adjoint.astype(jnp.bfloat16)[None]
    return (section_ends, section_starts, weight_part * factor, bias_part * factor)


def solution(mesh):
    placed = (
        P("layer"),
        P("layer", "sample", None, None, None),
        P("layer", "sample", None, None, None),
        P("layer", None, None, None),
        P("layer", None),
    )
    return jax.shard_map(
        body,
        mesh=mesh,
        in_specs=placed,
        out_specs=(
            P("layer", "sample", None, None, None),
            P("layer", "sample", None, None, None),
            P("layer", None, "sample", None),
            P("layer", "sample"),
        ),
        check_vma=False,
    )
```

profile of v0, /device:TPU:97, one launch (start us, length us, event | category | flops | bytes accessed | tf_op | source)
XLA Modules:
  0.0 226.4 jit_solution(11741997837996566327)
XLA Ops:
  8.0 0.8 slice_bitcast_fusion
  8.8 2.8 %pad_slice_fusion.120 = (bf16[1,32,32,128]{3,2,1,0:T(8,128)(2,1)S(1)}, bf16[1,32,32,128]{3,2,1,0:T(8,128)(2,1)S(1)}, bf16[1,32,32,128]{3,2,1,0:T(8,128)(2,1)S(1)...) fusion(bf16[1,32,32,128]{3,2,1,0:T(8,128)(2,1)} %bitcast.508), kind=kLoop, calls=%fused_computation.210 | loop fusion | bytes 2359296 | tf_op jit(solution)/shard_map/slice | solution.py:21
  11.7 0.6 slice_bitcast_fusion.7
  12.5 0.1 copy-done
  13.0 0.8 fusion.31
  13.9 0.3 pad_slice_fusion.112
  14.5 0.1 constant_dynamic-update-slice_fusion.13
  14.9 0.8 fusion.29
  15.7 0.1 fusion.126
  15.8 0.3 pad_slice_fusion.104
  16.4 0.2 constant_dynamic-update-slice_fusion.22
  16.9 0.8 fusion.27
  17.8 0.3 pad_slice_fusion.96
  18.4 0.2 constant_dynamic-update-slice_fusion.31
  18.9 0.8 fusion.25
  19.7 0.2 fusion.57
  19.9 5.5 %collective-permute-start = (bf16[1,32,32,128]{3,2,1,0:T(8,128)(2,1)S(1)}, bf16[1,32,32,128]{3,2,1,0:T(8,128)(2,1)S(1)}, u32[]{:S(2)}, u32[]{:S(2)}) collective-permute-start(bf16[1,32,32,128]{3,2,1,0:T(8,128)(2,1)S(1)} %fusion.57), channel_id=1, source_target_pairs={{0,16},{16,32},{32,48},{48,64},{64,80},{80,96},{96,112},{112,128},... | collective-permute-start | bytes 786440 | tf_op jit(solution)/shard_map/ppermute | solution.py:14
  25.5 0.9 copy.24
  26.4 0.9 copy.23
  27.3 0.9 copy.22
  28.2 0.9 copy.21
  29.1 0.9 convert_multiply_fusion
  31.0 1.6 broadcast_multiply_fusion.9
  32.6 2.5 %copy.25 = bf16[1024,1152]{0,1:T(8,128)(2,1)} copy(bf16[1024,1152]{1,0:T(8,128)(2,1)S(1)} %bitcast.501) | data formatting | bytes 4718592 | tf_op jit(solution)/shard_map/reshape | solution.py:25
  35.1 1.1 fusion.69
  36.7 0.1 constant_dynamic-update-slice_fusion.48
  37.1 1.8 broadcast_multiply_fusion.8
  38.9 2.5 %copy.26 = bf16[1024,1152]{0,1:T(8,128)(2,1)} copy(bf16[1024,1152]{1,0:T(8,128)(2,1)S(1)} %bitcast.503) | data formatting | bytes 4718592 | tf_op jit(solution)/shard_map/reshape | solution.py:25
  41.4 2.1 fusion.125
  44.5 1.6 broadcast_multiply_fusion.7
  46.1 2.5 %copy.27 = bf16[1024,1152]{0,1:T(8,128)(2,1)} copy(bf16[1024,1152]{1,0:T(8,128)(2,1)S(1)} %bitcast.505) | data formatting | bytes 4718592 | tf_op jit(solution)/shard_map/reshape | solution.py:25
  48.6 1.1 fusion.116
  50.2 0.1 constant_dynamic-update-slice_fusion.66
  50.7 1.8 broadcast_multiply_fusion.6
  52.5 2.5 %copy.28 = bf16[1024,1152]{0,1:T(8,128)(2,1)} copy(bf16[1024,1152]{1,0:T(8,128)(2,1)S(1)} %bitcast.507) | data formatting | bytes 4718592 | tf_op jit(solution)/shard_map/reshape | solution.py:25
  55.0 1.3 fusion.102
  56.8 0.1 constant_dynamic-update-slice_fusion.75
  57.3 0.8 broadcast_multiply_fusion.5
  59.2 0.8 broadcast_multiply_fusion.4
  61.1 0.8 broadcast_multiply_fusion.3
  62.5 0.1 constant_dynamic-update-slice_fusion.102
  63.0 0.8 fusion.52
  63.8 2.3 %collective-permute-start.1 = (bf16[1,32,32,128]{3,2,1,0:T(8,128)(2,1)S(1)}, bf16[1,32,32,128]{3,2,1,0:T(8,128)(2,1)S(1)}, u32[]{:S(2)}, u32[]{:S(2)}) collective-permute-start(bf16[1,32,32,128]{3,2,1,0:T(8,128)(2,1)S(1)} %fusion.52), channel_id=1, source_target_pairs={{16,0},{32,16},{48,32},{64,48},{80,64},{96,80},{112,96},{128,112},... | collective-permute-start | bytes 786440 | tf_op jit(solution)/shard_map/ppermute | solution.py:14
  66.1 0.9 fusion.110
  67.0 5.8 %collective-permute-done.1 = bf16[1,32,32,128]{3,2,1,0:T(8,128)(2,1)S(1)} collective-permute-done((bf16[1,32,32,128]{3,2,1,0:T(8,128)(2,1)S(1)}, bf16[1,32,32,128]{3,2,1,0:T(8,128)(2,1)S(1)}, u32[]{:S(2)}, u32[]{:S(2)}) %collective-permute-start.1) | collective-permute-done | bytes 262176 | tf_op jit(solution)/shard_map/ppermute | solution.py:14
  72.9 0.2 fusion.123
  73.1 1.5 fusion.51
  75.4 0.8 broadcast_multiply_fusion.2
  76.2 0.2 fusion.121
  76.4 0.7 copy-done.3
  77.1 1.5 fusion.50
  79.4 0.8 broadcast_multiply_fusion.1
  80.2 0.2 fusion.119
  80.4 0.7 copy-done.2
  81.1 1.5 fusion.49
  83.4 1.6 broadcast_multiply_fusion
  85.0 0.2 fusion.117
  85.2 33.6 %psum.15 = bf16[4,128]{1,0:T(4,128)(2,1)S(1)} all-reduce(bf16[4,128]{1,0:T(4,128)(2,1)S(1)} %pad_maximum_fusion.1), channel_id=1, replica_groups=mesh['layer'=16,'sample'=16] {'sample'}, use_global_device_ids=true, to_apply=%region_5.6 | all-reduce | flops 512 | bytes 2048 | tf_op jit(solution)/shard_map/psum | solution.py:101
  118.8 0.8 fusion.48
  119.5 2.3 %pad_maximum_fusion = bf16[4,9,128,128]{3,2,1,0:T(8,128)(2,1)} fusion(bf16[1,9,128,128]{3,2,1,0:T(8,128)(2,1)} %fusion.51, bf16[1,9,128,128]{3,2,1,0:T(8,128)(2,1)} %fusion.50, bf16[1,9,128,128]{3,2,1,0:T(8,128)(2,1)} %fusion.49, bf16[1,9,128,128]{3,2,1,0:T(8,128)(2,1)S(1)} %fusion.48), kind=kLoop, calls=%fused_computation.46 | loop fusion | flops 1769472 | bytes 2359296 | tf_op jit(solution)/shard_map/stack | solution.py:73
  122.1 0.7 dynamic-slice_multiply_fusion
  123.4 1.5 fusion.53
  124.9 93.1 %all-reduce.18.cloned.1.call-done = bf16[4,9,128,128]{3,2,1,0:T(8,128)(2,1)} async-done(((bf16[4,9,128,128]{3,2,1,0:T(8,128)(2,1)}), bf16[4,9,128,128]{3,2,1,0:T(8,128)(2,1)}) %all-reduce.18.cloned.1.call-update) | async-done | bytes 1179664 | tf_op jit(solution)/shard_map/psum | solution.py:100
  218.0 1.6 convert_multiply_fusion.2
  (196 shorter events, 13.0 us)
Async XLA Ops:
  7.2 4.5 %copy-start.17 = (bf16[4,9,128,128]{3,2,1,0:T(8,128)(2,1)S(1)}, bf16[4,9,128,128]{3,2,1,0:T(8,128)(2,1)}, u32[]{:S(2)}) copy-start(bf16[4,9,128,128]{3,2,1,0:T(8,128)(2,1)} %param.8) | copy-start | bytes 3538948
  7.2 210.9 %all-reduce.18.cloned.1.call-start = ((), (), s32[]{:S(2)}) async-start(), calls=%async_computation | async-start | bytes 2359296 | tf_op jit(solution)/shard_map/psum | solution.py:100
  11.7 1.0 copy-start
  12.2 1.5 copy-start.22
  12.3 4.6 %copy-start.20 = (bf16[1,9,128,128]{3,2,1,0:T(8,128)(2,1)}, bf16[1,9,128,128]{3,2,1,0:T(8,128)(2,1)S(1)}, u32[]{:S(2)}) copy-start(bf16[1,9,128,128]{3,2,1,0:T(8,128)(2,1)S(1)} %get-tuple-element.23) | copy-start | bytes 884740
  12.3 6.6 %copy-start.18 = (bf16[1,9,128,128]{3,2,1,0:T(8,128)(2,1)}, bf16[1,9,128,128]{3,2,1,0:T(8,128)(2,1)S(1)}, u32[]{:S(2)}) copy-start(bf16[1,9,128,128]{3,2,1,0:T(8,128)(2,1)S(1)} %get-tuple-element.22) | copy-start | bytes 884740
  19.9 10.1 %collective-permute-start = (bf16[1,32,32,128]{3,2,1,0:T(8,128)(2,1)S(1)}, bf16[1,32,32,128]{3,2,1,0:T(8,128)(2,1)S(1)}, u32[]{:S(2)}, u32[]{:S(2)}) collective-permute-start(bf16[1,32,32,128]{3,2,1,0:T(8,128)(2,1)S(1)} %fusion.57), channel_id=1, source_target_pairs={{0,16},{16,32},{32,48},{48,64},{64,80},{80,96},{96,112},{112,128},... | collective-permute-start | bytes 786440 | tf_op jit(solution)/shard_map/ppermute | solution.py:14
  25.4 3.8 %copy-start.9 = (bf16[1,1,32,32,128]{4,3,2,1,0:T(8,128)(2,1)S(1)}, bf16[1,1,32,32,128]{4,3,2,1,0:T(8,128)(2,1)}, u32[]{:S(2)}) copy-start(bf16[1,1,32,32,128]{4,3,2,1,0:T(8,128)(2,1)} %param.7) | copy-start | bytes 786436
  30.0 1.0 copy-start.23
  43.5 1.0 copy-start.21
  49.7 1.0 copy-start.19
  56.3 1.0 copy-start.10
  56.3 1.0 copy-start.15
  57.1 1.1 copy-start.6
  58.2 1.0 copy-start.13
  59.0 1.1 copy-start.5
  60.2 1.0 copy-start.12
  62.0 1.0 copy-start.14
  62.7 3.4 %copy-start.8 = (f32[1,32,32,128]{3,2,1,0:T(8,128)S(1)}, f32[1,32,32,128]{3,2,1,0:T(8,128)}, u32[]{:S(2)}) copy-start(f32[1,32,32,128]{3,2,1,0:T(8,128)} %get-tuple-element.13) | copy-start | bytes 1572868
  62.7 3.4 %copy-start.11 = (f32[1024,128]{1,0:T(8,128)S(1)}, f32[1024,128]{1,0:T(8,128)}, u32[]{:S(2)}) copy-start(f32[1024,128]{1,0:T(8,128)} %get-tuple-element.66) | copy-start | bytes 1572868
  63.0 9.9 %copy-start.7 = (f32[1024,128]{1,0:T(8,128)S(1)}, f32[1024,128]{1,0:T(8,128)}, u32[]{:S(2)}) copy-start(f32[1024,128]{1,0:T(8,128)} %get-tuple-element.67) | copy-start | bytes 1572868
  63.8 9.3 %copy-start.4 = (bf16[1024,1152]{0,1:T(8,128)(2,1)S(1)}, bf16[1024,1152]{0,1:T(8,128)(2,1)}, u32[]{:S(2)}) copy-start(bf16[1024,1152]{0,1:T(8,128)(2,1)} %copy.28) | copy-start | bytes 7077892
  63.8 9.0 %collective-permute-start.1 = (bf16[1,32,32,128]{3,2,1,0:T(8,128)(2,1)S(1)}, bf16[1,32,32,128]{3,2,1,0:T(8,128)(2,1)S(1)}, u32[]{:S(2)}, u32[]{:S(2)}) collective-permute-start(bf16[1,32,32,128]{3,2,1,0:T(8,128)(2,1)S(1)} %fusion.52), channel_id=1, source_target_pairs={{16,0},{32,16},{48,32},{64,48},{80,64},{96,80},{112,96},{128,112},... | collective-permute-start | bytes 786440 | tf_op jit(solution)/shard_map/ppermute | solution.py:14
  75.4 1.7 copy-start.3
  79.4 1.7 copy-start.2
  83.4 35.4 %copy-start.1 = (bf16[1024,1152]{0,1:T(8,128)(2,1)S(1)}, bf16[1024,1152]{0,1:T(8,128)(2,1)}, u32[]{:S(2)}) copy-start(bf16[1024,1152]{0,1:T(8,128)(2,1)} %copy.25) | copy-start | bytes 7077892
  121.9 1.5 copy-start.16
Sparse Core Ops, SparseCore 0:
  122.0 95.9 all-reduce.17
where the time goes:
time: 229 us; the launch traced here: 226 us
  waiting for transfers between devices  99 us (43%)
  blocking collectives  33.6 us (15%)
  local copies, waits for them, and re-layouts  33.2 us (14%)
  matrix products  22.9 us (10%)
  between operations  16 us (7%)
  other arithmetic  13.9 us (6%)
  starting transfers between devices  7.84 us (3%)
    psum x1, waiting for transfers between devices, body(): lax.psum(weight_terms.astype(jnp.bfloat16), 'sample').astype(jnp.float32)  93.1 us
    psum x1, blocking collectives, body(): lax.psum(bias_terms.astype(jnp.bfloat16), 'sample').astype(jnp.float32)  33.6 us
    unnamed x173, local copies, waits for them, and re-layouts  12.7 us
    reshape x4, local copies, waits for them, and re-layouts, patches(): return jnp.concatenate(windows, axis=-1).reshape(-1, 9 * channels)  10.1 us
    dot_general x8, matrix products, run_section(): jnp.dot(windows, weights[layer_pos].reshape(9 * channels, channels), pref...  9.91 us
    ppermute x2, starting transfers between devices, from_behind(): return lax.ppermute(block, axis, route)  7.81 us
    dot_general x8, matrix products, back_section(): jnp.dot(patches(signal.reshape(adjoint.shape)), flipped, preferred_elemen...  7.74 us
    ppermute x2, waiting for transfers between devices, from_behind(): return lax.ppermute(block, axis, route)  5.82 us
  transfers between devices with their start and end apart: 3, of which 2 were waited for; matrix products, arithmetic and copies ran while one was open for 4% of the time, Pallas kernels for 0%

commit v1 on v0

v1 whole, which is shorter than its diff:
```python
import functools
import math

import jax
import jax.numpy as jnp
from jax import lax
from jax.experimental import pallas as pl
from jax.experimental.pallas import tpu as pltpu
from jax.sharding import PartitionSpec as P

STEP_SIZE = 0.5
C = 128
LMAX = 4
TAPS = 9
F32 = jnp.float32
BF16 = jnp.bfloat16
LEFT = 8


def shift_by(block, axis, distance):
    devices = range(lax.axis_size(axis))
    route = [(i - distance, i) for i in devices if i - distance in devices]
    return lax.ppermute(block, axis, route)


def clear_edges(wide, fan):
    edge = jnp.zeros((16, 2, 8, C), F32)
    wide[:, :, 0:8, :] = edge
    wide[:, :, 40:48, :] = edge
    line = jnp.zeros((32, 3 * C), BF16)
    fan[0, 0] = line
    fan[16, 1] = line


def spread(wide, fan):
    for dx in range(3):
        lanes = slice(dx * C, (dx + 1) * C)
        columns = slice(LEFT - 1 + dx, LEFT + 31 + dx)
        fan[0:16, 1, :, lanes] = wide[:, 0, columns, :].astype(BF16)
        fan[1:17, 0, :, lanes] = wide[:, 1, columns, :].astype(BF16)


def row_window(fan, row, lanes=slice(0, 3 * C)):
    return fan[row // 2 : row // 2 + 16, row % 2, :, lanes].reshape(512, -1)


def convolve(fan, matrix, transposed):
    rows = jnp.concatenate([row_window(fan, row) for row in range(4)], axis=1)
    dims = (((1,), (1 if transposed else 0,)), ((), ()))
    return lax.dot_general(rows, matrix, dims, preferred_element_type=F32)


def forward_matrix(w):
    zero = jnp.zeros((C, C), BF16)
    columns = []
    for out in range(2):
        blocks = [
            w[3 * (row - out) + dx] if 0 <= row - out <= 2 else zero
            for row in range(4)
            for dx in range(3)
        ]
        columns.append(jnp.concatenate(blocks, axis=0))
    return jnp.concatenate(columns, axis=1)


def backward_matrix(w):
    zero = jnp.zeros((C, C), BF16)
    rows = []
    for out in range(2):
        blocks = [
            w[8 - 3 * (row - out) - dx] if 0 <= row - out <= 2 else zero
            for row in range(4)
            for dx in range(3)
        ]
        rows.append(jnp.concatenate(blocks, axis=1))
    return jnp.concatenate(rows, axis=0)


def forward_layer(w, bias, wide, fan, slope=None):
    z = convolve(fan, forward_matrix(w), False) + jnp.concatenate([bias, bias], axis=1)
    t = jnp.tanh(z)
    for half in range(2):
        part = t[:, half * C : (half + 1) * C].reshape(16, 32, C)
        wide[:, half, LEFT : LEFT + 32, :] += STEP_SIZE * part
        if slope is not None:
            slope[:, half] = STEP_SIZE * (1.0 - part * part)


def backward_layer(w, wide, fan, adjoint, slope):
    wide[:, :, LEFT : LEFT + 32, :] = adjoint[...] * slope[...]
    spread(wide, fan)
    back = convolve(fan, backward_matrix(w), True)
    for half in range(2):
        adjoint[:, half] += back[:, half * C : (half + 1) * C].reshape(16, 32, C)


def first_kernel(length, state, w, bias, out, wide, fan):
    j = pl.program_id(0)

    @pl.when(j == 0)
    def _():
        clear_edges(wide, fan)
        wide[:, :, LEFT : LEFT + 32, :] = state[...].astype(F32)

    @pl.when(j < length[0])
    def _():
        spread(wide, fan)
        forward_layer(w.at[0], bias[pl.ds(j, 1), :], wide, fan)

    @pl.when(j == LMAX - 1)
    def _():
        out[...] = wide[:, :, LEFT : LEFT + 32, :].astype(BF16)


def second_kernel(
    length, given, received, terminal, w, bias, ending, back, states, slopes, wide, fan, kept, adjoint
):
    step = pl.program_id(0)
    leading = lax.axis_index("layer") == 0

    @pl.when(step == 0)
    def _():
        clear_edges(wide, fan)
        adjoint[...] = terminal[...].astype(F32)

    @pl.when(jnp.logical_and(step == 0, leading))
    def _():
        wide[:, :, LEFT : LEFT + 32, :] = given[...].astype(F32)

    @pl.when(jnp.logical_and(step == 0, jnp.logical_not(leading)))
    def _():
        wide[:, :, LEFT : LEFT + 32, :] = received[...].astype(F32)

    @pl.when(step < length[0])
    def _():
        spread(wide, fan)
        states[0, :, 0] = fan[0:16, 1, :, C : 2 * C]
        states[0, :, 1] = fan[1:17, 0, :, C : 2 * C]
        forward_layer(w.at[0], bias[pl.ds(step, 1), :], wide, fan, kept.at[step])
        slopes[0] = kept[step]

    @pl.when(step == LMAX - 1)
    def _():
        ending[...] = wide[:, :, LEFT : LEFT + 32, :].astype(BF16)

    slot = 2 * LMAX - 1 - step

    @pl.when(jnp.logical_and(step >= LMAX, slot < length[0]))
    def _():
        backward_layer(w.at[0], wide, fan, adjoint, kept.at[slot])

    @pl.when(step == 2 * LMAX - 1)
    def _():
        back[...] = adjoint[...].astype(BF16)


def turn_kernel(length, states, turned, wide):
    j = pl.program_id(0)

    @pl.when(j == 0)
    def _():
        edge = jnp.zeros((16, 2, 8, C), F32)
        wide[:, :, 0:8, :] = edge
        wide[:, :, 40:48, :] = edge

    @pl.when(j < length[0])
    def _():
        wide[:, :, LEFT : LEFT + 32, :] = states[0].astype(F32)
        for dx in range(3):
            for half in range(2):
                part = wide[:, half, LEFT - 1 + dx : LEFT + 31 + dx, :].reshape(512, C)
                turned[0, dx * C : (dx + 1) * C, half * 512 : (half + 1) * 512] = part.astype(BF16).T


def third_kernel(
    length, given, received, w, turned, slopes, start, grads, wide, fan, adjoint, sums
):
    step = pl.program_id(0)
    slot = LMAX - 1 - step
    trailing = lax.axis_index("layer") == lax.axis_size("layer") - 1

    @pl.when(step == 0)
    def _():
        clear_edges(wide, fan)
        sums[...] = jnp.zeros_like(sums)

    @pl.when(jnp.logical_and(step == 0, trailing))
    def _():
        adjoint[...] = given[...].astype(F32)

    @pl.when(jnp.logical_and(step == 0, jnp.logical_not(trailing)))
    def _():
        adjoint[...] = received[...].astype(F32)

    @pl.when(slot < length[0])
    def _():
        backward_layer(w.at[0], wide, fan, adjoint, slopes.at[0])
        middle = slice(C, 2 * C)
        signals = jnp.concatenate(
            [
                jnp.concatenate([row_window(fan, half + 2 - dy, middle) for dy in range(3)], axis=1)
                for half in range(2)
            ],
            axis=0,
        )
        total = jnp.dot(turned[0], signals, preferred_element_type=F32)
        for dy in range(3):
            for dx in range(3):
                block = total[dx * C : (dx + 1) * C, dy * C : (dy + 1) * C]
                grads[:, slot * TAPS + 3 * dy + dx] = block.reshape(16, 8, C).astype(BF16)
        sums[pl.ds(slot, 1), :] = jnp.sum(
            signals[:, C : 2 * C].astype(F32), axis=0, keepdims=True
        )

    @pl.when(slot >= length[0])
    def _():
        grads[:, pl.ds(slot * TAPS, TAPS)] = jnp.zeros((16, TAPS, 8, C), BF16)

    @pl.when(step == LMAX - 1)
    def _():
        start[...] = adjoint[...].astype(BF16)
        grads[:, LMAX * TAPS] = jnp.broadcast_to(sums[...][None], (16, 8, C)).astype(BF16)


IMAGE = (16, 2, 32, C)
WIDE = pltpu.VMEM((16, 2, 48, C), F32)
FAN = pltpu.VMEM((17, 2, 32, 3 * C), BF16)
CONV_FLOPS = 2 * 1024 * 9 * C * C


def whole(shape):
    return pl.BlockSpec(shape, lambda *_: (0,) * len(shape))


def slotted(shape, slot_of):
    rest = (0,) * len(shape)
    return pl.BlockSpec((1,) + shape, lambda step, *_: (slot_of(step),) + rest)


def call(kernel, name, steps, ins, outs, shapes, scratch, flops):
    return pl.pallas_call(
        kernel,
        name=name,
        out_shape=shapes,
        grid_spec=pltpu.PrefetchScalarGridSpec(
            num_scalar_prefetch=1, grid=(steps,), in_specs=ins, out_specs=outs, scratch_shapes=scratch
        ),
        compiler_params=pltpu.CompilerParams(
            dimension_semantics=("arbitrary",), vmem_limit_bytes=40 * 2**20
        ),
        cost_estimate=pl.CostEstimate(flops=flops, bytes_accessed=4 * 2**20, transcendentals=0),
    )


def body(section_lengths, forward_states, adjoint_states, weights, biases):
    given_state = forward_states.reshape(IMAGE)
    given_adjoint = adjoint_states.reshape(IMAGE)
    image = jax.ShapeDtypeStruct(IMAGE, BF16)
    taps = (TAPS, C, C)
    up = slotted(taps, lambda step: step)
    down = slotted(taps, lambda step: LMAX - 1 - step)

    propagated = call(
        first_kernel, "first", LMAX,
        [whole(IMAGE), up, whole((LMAX, C))],
        whole(IMAGE), image, [WIDE, FAN], LMAX * CONV_FLOPS,
    )(section_lengths, given_state, weights, biases)
    received = shift_by(propagated, "layer", 1)

    ending, back_start, states, slopes = call(
        second_kernel, "second", 2 * LMAX,
        [
            whole(IMAGE), whole(IMAGE), whole(IMAGE),
            slotted(taps, lambda step: jnp.minimum(step, 2 * LMAX - 1 - step)),
            whole((LMAX, C)),
        ],
        [
            whole(IMAGE), whole(IMAGE),
            slotted(IMAGE, lambda step: jnp.minimum(step, LMAX - 1)),
            slotted(IMAGE, lambda step: jnp.minimum(step, LMAX - 1)),
        ],
        [
            image, image,
            jax.ShapeDtypeStruct((LMAX,) + IMAGE, BF16),
            jax.ShapeDtypeStruct((LMAX,) + IMAGE, F32),
        ],
        [WIDE, FAN, pltpu.VMEM((LMAX,) + IMAGE, F32), pltpu.VMEM(IMAGE, F32)],
        2 * LMAX * CONV_FLOPS,
    )(section_lengths, given_state, received, given_adjoint, weights, biases)
    received_back = shift_by(back_start, "layer", -1)

    turned = call(
        turn_kernel, "turn", LMAX,
        [slotted(IMAGE, lambda step: step)],
        slotted((3 * C, 1024), lambda step: step),
        jax.ShapeDtypeStruct((LMAX, 3 * C, 1024), BF16),
        [WIDE], 10**6,
    )(section_lengths, states)

    starting, grads = call(
        third_kernel, "third", LMAX,
        [
            whole(IMAGE), whole(IMAGE), down,
            slotted((3 * C, 1024), lambda step: LMAX - 1 - step),
            slotted(IMAGE, lambda step: LMAX - 1 - step),
        ],
        [whole(IMAGE), whole((16, LMAX * TAPS + 1, 8, C))],
        [image, jax.ShapeDtypeStruct((16, LMAX * TAPS + 1, 8, C), BF16)],
        [WIDE, FAN, pltpu.VMEM(IMAGE, F32), pltpu.VMEM((8, C), F32)],
        2 * LMAX * CONV_FLOPS,
    )(section_lengths, given_adjoint, received_back, weights, turned, slopes)

    pieces = lax.all_to_all(grads, "sample", 0, 0)
    total_samples = forward_states.shape[1] * lax.axis_size("sample")
    factor = 1.0 / math.sqrt(total_samples * forward_states.shape[2] * forward_states.shape[3])
    total = jnp.sum(pieces.astype(F32), axis=0) * factor
    weight_part = total[: LMAX * TAPS].reshape(LMAX, TAPS, 8, C)
    bias_part = lax.dynamic_slice_in_dim(total[LMAX * TAPS, :LMAX], 8 * lax.axis_index("sample"), 8, 1)
    shape = forward_states.shape
    return (ending.reshape(shape), starting.reshape(shape), weight_part, bias_part)


def solution(mesh):
    placed = (
        P("layer"),
        P("layer", "sample", None, None, None),
        P("layer", "sample", None, None, None),
        P("layer", None, None, None),
        P("layer", None),
    )
    return jax.shard_map(
        body,
        mesh=mesh,
        in_specs=placed,
        out_specs=(
            P("layer", "sample", None, None, None),
            P("layer", "sample", None, None, None),
            P("layer", None, "sample", None),
            P("layer", "sample"),
        ),
        check_vma=False,
    )
```

time: 229 us -> 62.2 us (0.27); the launches traced: 226 us -> 63.4 us
  waiting for transfers between devices: 99 us -> 32.2 us
  blocking collectives: 33.6 us -> 0 us
  local copies, waits for them, and re-layouts: 33.2 us -> 4.23 us
  matrix products: 22.9 us -> 0 us
  between operations: 16 us -> 1.35 us
  other arithmetic: 13.9 us -> 0.18 us
  starting transfers between devices: 7.84 us -> 19.2 us
  Pallas kernels: 0 us -> 6.21 us
    psum x1 -> x0, waiting for transfers between devices: 93.1 us -> none  [body(): lax.psum(weight_terms.astype(jnp.bfloat16), 'sample').astype(jnp.float32)]
    psum x1 -> x0, blocking collectives: 33.6 us -> none  [body(): lax.psum(bias_terms.astype(jnp.bfloat16), 'sample').astype(jnp.float32)]
    dot_general x20 -> x0, matrix products: 22.9 us -> none  [the longest x8 9.91 us: run_section(): jnp.dot(windows, weights[layer_pos].reshape(9 * channels, channels), pref...]
    all_to_all x0 -> x1, waiting for transfers between devices: none -> 21.3 us  [body(): pieces = lax.all_to_all(grads, 'sample', 0, 0)]
    reshape x4 -> x0, local copies, waits for them, and re-layouts: 10.1 us -> none  [patches(): return jnp.concatenate(windows, axis=-1).reshape(-1, 9 * channels)]
    unnamed x173 -> x10, local copies, waits for them, and re-layouts: 12.7 us -> 2.91 us
    all_to_all x0 -> x1, starting transfers between devices: none -> 6.74 us  [body(): pieces = lax.all_to_all(grads, 'sample', 0, 0)]
    pallas_call x0 -> x4, Pallas kernels: none -> 6.21 us  [the longest x1 2.55 us: body(): call(second_kernel, 'second', 2 * LMAX, [whole(IMAGE), whole(IMAGE), whol...]
  transfers between devices with their start and end apart: 3 -> 3, of which waited for: 2 -> 3; matrix products, arithmetic and copies ran while one was open for 4% -> 0% of each run, Pallas kernels for 0% -> 1%
where the time goes in v1:
time: 62.2 us; the launch traced here: 63.4 us
  waiting for transfers between devices  32.2 us (52%)
  starting transfers between devices  19.2 us (31%)
  Pallas kernels  6.21 us (10%)
  local copies, waits for them, and re-layouts  4.23 us (7%)
  between operations  1.35 us (2%)
    all_to_all x1, waiting for transfers between devices, body(): pieces = lax.all_to_all(grads, 'sample', 0, 0)  21.3 us
    ppermute x2, starting transfers between devices, shift_by(): return lax.ppermute(block, axis, route)  12.5 us
    ppermute x2, waiting for transfers between devices, shift_by(): return lax.ppermute(block, axis, route)  10.9 us
    all_to_all x1, starting transfers between devices, body(): pieces = lax.all_to_all(grads, 'sample', 0, 0)  6.74 us
    unnamed x10, local copies, waits for them, and re-layouts  2.91 us
    pallas_call x1, Pallas kernels, body(): call(second_kernel, 'second', 2 * LMAX, [whole(IMAGE), whole(IMAGE), whol...  2.55 us
    pallas_call x1, Pallas kernels, body(): call(third_kernel, 'third', LMAX, [whole(IMAGE), whole(IMAGE), down, slot...  2.51 us
  transfers between devices with their start and end apart: 3, of which 3 were waited for; matrix products, arithmetic and copies ran while one was open for 0% of the time, Pallas kernels for 1%

profile of v1, /device:TPU:97, one launch (start us, length us, event | category | flops | bytes accessed | tf_op | source)
XLA Modules:
  0.0 63.4 jit_solution(15284563787751724161)
XLA Ops:
  1.3 0.0 copy-start
  1.3 1.3 %copy-done = bf16[4,9,128,128]{3,2,1,0:T(8,128)(2,1)S(1)} copy-done((bf16[4,9,128,128]{3,2,1,0:T(8,128)(2,1)S(1)}, bf16[4,9,128,128]{3,2,1,0:T(8,128)(2,1)}, u32[]{:S(2)}) %copy-start) | copy-done | bytes 1179672
  2.6 0.0 copy-start.2
  2.6 0.9 %copy-done.2 = bf16[1,1,32,32,128]{4,3,2,1,0:T(8,128)(2,1)S(1)} copy-done((bf16[1,1,32,32,128]{4,3,2,1,0:T(8,128)(2,1)S(1)}, bf16[1,1,32,32,128]{4,3,2,1,0:T(8,128)(2,1)}, u32[]{:S(2)}) %copy-start.2) | copy-done | bytes 262168
  3.5 0.0 copy-start.4
  3.5 0.7 %copy-done.4 = f32[4,128]{1,0:T(4,128)S(1)} copy-done((f32[4,128]{1,0:T(4,128)S(1)}, f32[4,128]{1,0:T(4,128)}, u32[]{:S(2)}) %copy-start.4) | copy-done | bytes 2072
  4.2 0.0 copy-start.3
  4.2 0.8 %first.1 = bf16[16,2,32,128]{3,2,1,0:T(8,128)(2,1)S(1)} custom-call(s32[1]{0:T(128)S(6)} %copy.9.length, bf16[16,2,32,128]{3,2,1,0:T(8,128)(2,1)S(1)} %bitcast.7, bf16[4,9,128,128]{3,2,1,0:T(8,128)(2,1)S(1)} %copy-done, f32[4,128]{1,0:T(4,128)S(1)} %copy-done.4), custom_call_target="tpu_custom_call" | custom-call | flops 1207959552 | bytes 4194304 | tf_op jit(solution)/shard_map/first/pallas_call | solution.py:263
  5.0 7.1 %collective-permute-start = (bf16[16,2,32,128]{3,2,1,0:T(8,128)(2,1)S(1)}, bf16[16,2,32,128]{3,2,1,0:T(8,128)(2,1)S(1)}, u32[]{:S(2)}, u32[]{:S(2)}) collective-permute-start(bf16[16,2,32,128]{3,2,1,0:T(8,128)(2,1)S(1)} %first.1), channel_id=1, source_target_pairs={{0,16},{16,32},{32,48},{48,64},{64,80},{80,96},{96,112},{112,128},... | collective-permute-start | bytes 786440 | tf_op jit(solution)/shard_map/ppermute | solution.py:23
  12.1 3.3 %collective-permute-done.received = bf16[16,2,32,128]{3,2,1,0:T(8,128)(2,1)S(1)} collective-permute-done((bf16[16,2,32,128]{3,2,1,0:T(8,128)(2,1)S(1)}, bf16[16,2,32,128]{3,2,1,0:T(8,128)(2,1)S(1)}, u32[]{:S(2)}, u32[]{:S(2)}) %collective-permute-start) | collective-permute-done | bytes 262176 | tf_op jit(solution)/shard_map/ppermute | solution.py:23
  15.4 0.0 copy-done.3
  15.4 2.5 %second.1 = (bf16[16,2,32,128]{3,2,1,0:T(8,128)(2,1)}, bf16[16,2,32,128]{3,2,1,0:T(8,128)(2,1)S(1)}, bf16[4,16,2,32,128]{4,3,2,1,0:T(8,128)(2,1)S(1)}, f32[4,16,2,32,128]{4,3,2,1,0:T(8,128)S(1)}) custom-call(s32[1]{0:T(128)S(6)} %copy.9.length, bf16[16,2,32,128]{3,2,1,0:T(8,128)(2,1)S(1)} %bitcast.8, ...), custom_call_target="tpu_custom_call" | custom-call | flops 2415919104 | bytes 4194304 | tf_op jit(solution)/shard_map/second/pallas_call | solution.py:270
  17.9 5.4 %collective-permute-start.1 = (bf16[16,2,32,128]{3,2,1,0:T(8,128)(2,1)S(1)}, bf16[16,2,32,128]{3,2,1,0:T(8,128)(2,1)S(1)}, u32[]{:S(2)}, u32[]{:S(2)}) collective-permute-start(bf16[16,2,32,128]{3,2,1,0:T(8,128)(2,1)S(1)} %get-tuple-element.11), channel_id=1, source_target_pairs={{16,0},{32,16},{48,32},{64,48},{80,64},{96,80},{112,96},{128,112},... | collective-permute-start | bytes 786440 | tf_op jit(solution)/shard_map/ppermute | solution.py:23
  23.3 0.0 copy-start.1
  23.3 0.4 turn.1.turned
  23.7 7.6 %collective-permute-done.1.received = bf16[16,2,32,128]{3,2,1,0:T(8,128)(2,1)S(1)} collective-permute-done((bf16[16,2,32,128]{3,2,1,0:T(8,128)(2,1)S(1)}, bf16[16,2,32,128]{3,2,1,0:T(8,128)(2,1)S(1)}, u32[]{:S(2)}, u32[]{:S(2)}) %collective-permute-start.1) | collective-permute-done | bytes 262176 | tf_op jit(solution)/shard_map/ppermute | solution.py:23
  31.3 0.0 copy-done.1
  31.3 2.5 %third.1 = (bf16[16,2,32,128]{3,2,1,0:T(8,128)(2,1)}, bf16[16,37,8,128]{3,2,1,0:T(8,128)(2,1)}) custom-call(s32[1]{0:T(128)S(6)} %copy.9.length, bf16[16,2,32,128]{3,2,1,0:T(8,128)(2,1)S(1)} %bitcast.10, bf16[16,2,32,128]{3,2,1,0:T(8,128)(2,1)S(1)} %collective-permute-done.1.received, bf16[4,9,128,128]{3,2,1,0:T(8,128)(2,1)S(1)} %copy-done.1, ...), custom_call_target="tpu_custom_call" | custom-call | flops 2415919104 | bytes 4194304 | tf_op jit(solution)/shard_map/third/pallas_call | solution.py:300
  33.8 6.7 %all-to-all-start = ((bf16[16,37,8,128]{3,2,1,0:T(8,128)(2,1)}), bf16[16,37,8,128]{3,2,1,0:T(8,128)(2,1)S(1)}, u32[]{:S(2)}, u32[]{:S(2)}) async-start(bf16[16,37,8,128]{3,2,1,0:T(8,128)(2,1)} %get-tuple-element.15), calls=%async_computation | async-start | bytes 2424832 | tf_op jit(solution)/shard_map/all_to_all | solution.py:313
  40.6 21.3 %all-to-all-done = bf16[16,37,8,128]{3,2,1,0:T(8,128)(2,1)S(1)} async-done(((bf16[16,37,8,128]{3,2,1,0:T(8,128)(2,1)}), bf16[16,37,8,128]{3,2,1,0:T(8,128)(2,1)S(1)}, u32[]{:S(2)}, u32[]{:S(2)}) %all-to-all-start) | async-done | bytes 1212448 | tf_op jit(solution)/shard_map/all_to_all | solution.py:313
  61.8 0.2 convert_reduce_fusion
  62.0 0.7 %slice.8 = f32[36,8,128]{2,1,0:T(8,128)} slice(f32[37,8,128]{2,1,0:T(8,128)S(1)} %broadcast_multiply_fusion), slice={[0:36], [0:8], [0:128]} | slice | bytes 294912 | tf_op jit(solution)/shard_map/slice | solution.py:317
  62.7 0.7 %dynamic-slice_bitcast_fusion = f32[4,8]{1,0:T(4,128)} fusion(f32[1,4,128]{2,1,0:T(4,128)S(1)} %slice.9, s32[]{:T(128)S(6)} %select_n.3), kind=kLoop, calls=%fused_computation.2 | loop fusion | bytes 260 | tf_op jit(solution)/shard_map/dynamic_slice | solution.py:318
  (2 shorter events, 0.0 us)
Async XLA Ops:
  1.3 1.3 %copy-start = (bf16[4,9,128,128]{3,2,1,0:T(8,128)(2,1)S(1)}, bf16[4,9,128,128]{3,2,1,0:T(8,128)(2,1)}, u32[]{:S(2)}) copy-start(bf16[4,9,128,128]{3,2,1,0:T(8,128)(2,1)} %w.5) | copy-start | bytes 3538948
  2.6 0.9 %copy-start.2 = (bf16[1,1,32,32,128]{4,3,2,1,0:T(8,128)(2,1)S(1)}, bf16[1,1,32,32,128]{4,3,2,1,0:T(8,128)(2,1)}, u32[]{:S(2)}) copy-start(bf16[1,1,32,32,128]{4,3,2,1,0:T(8,128)(2,1)} %param.6) | copy-start | bytes 786436
  3.5 0.7 %copy-start.4 = (f32[4,128]{1,0:T(4,128)S(1)}, f32[4,128]{1,0:T(4,128)}, u32[]{:S(2)}) copy-start(f32[4,128]{1,0:T(4,128)} %bias.3) | copy-start | bytes 6148
  4.2 11.2 %copy-start.3 = (bf16[1,1,32,32,128]{4,3,2,1,0:T(8,128)(2,1)S(1)}, bf16[1,1,32,32,128]{4,3,2,1,0:T(8,128)(2,1)}, u32[]{:S(2)}) copy-start(bf16[1,1,32,32,128]{4,3,2,1,0:T(8,128)(2,1)} %param.7) | copy-start | bytes 786436
  5.0 10.4 %collective-permute-start = (bf16[16,2,32,128]{3,2,1,0:T(8,128)(2,1)S(1)}, bf16[16,2,32,128]{3,2,1,0:T(8,128)(2,1)S(1)}, u32[]{:S(2)}, u32[]{:S(2)}) collective-permute-start(bf16[16,2,32,128]{3,2,1,0:T(8,128)(2,1)S(1)} %first.1), channel_id=1, source_target_pairs={{0,16},{16,32},{32,48},{48,64},{64,80},{80,96},{96,112},{112,128},... | collective-permute-start | bytes 786440 | tf_op jit(solution)/shard_map/ppermute | solution.py:23
  17.9 13.4 %collective-permute-start.1 = (bf16[16,2,32,128]{3,2,1,0:T(8,128)(2,1)S(1)}, bf16[16,2,32,128]{3,2,1,0:T(8,128)(2,1)S(1)}, u32[]{:S(2)}, u32[]{:S(2)}) collective-permute-start(bf16[16,2,32,128]{3,2,1,0:T(8,128)(2,1)S(1)} %get-tuple-element.11), channel_id=1, source_target_pairs={{16,0},{32,16},{48,32},{64,48},{80,64},{96,80},{112,96},{128,112},... | collective-permute-start | bytes 786440 | tf_op jit(solution)/shard_map/ppermute | solution.py:23
  23.3 8.0 %copy-start.1 = (bf16[4,9,128,128]{3,2,1,0:T(8,128)(2,1)S(1)}, bf16[4,9,128,128]{3,2,1,0:T(8,128)(2,1)}, u32[]{:S(2)}) copy-start(bf16[4,9,128,128]{3,2,1,0:T(8,128)(2,1)} %w.5) | copy-start | bytes 3538948
  33.8 28.0 %all-to-all-start = ((bf16[16,37,8,128]{3,2,1,0:T(8,128)(2,1)}), bf16[16,37,8,128]{3,2,1,0:T(8,128)(2,1)S(1)}, u32[]{:S(2)}, u32[]{:S(2)}) async-start(bf16[16,37,8,128]{3,2,1,0:T(8,128)(2,1)} %get-tuple-element.15), calls=%async_computation | async-start | bytes 2424832 | tf_op jit(solution)/shard_map/all_to_all | solution.py:313

commit v2 on v1

v2 whole, which is shorter than its diff:
```python
import functools
import math

import jax
import jax.numpy as jnp
from jax import lax
from jax.experimental import pallas as pl
from jax.experimental.pallas import tpu as pltpu
from jax.sharding import PartitionSpec as P


STEP_SIZE = 0.5
C = 128
LMAX = 4
HALF = 2
SIDE = 4
TAPS = 9
F32 = jnp.float32
BF16 = jnp.bfloat16
LEFT = 8


def shift_by(block, axis, distance):
    count = lax.axis_size(axis)
    return lax.ppermute(block, axis, [(i, (i + distance) % count) for i in range(count)])


def send_ahead(block, along_x, distance):
    route = []
    for y in range(SIDE):
        for x in range(SIDE):
            to = (y, (x + distance) % SIDE) if along_x else ((y + distance) % SIDE, x)
            route.append((SIDE * y + x, SIDE * to[0] + to[1]))
    return lax.ppermute(block, "sample", route)


def clear_edges(wide, fan):
    edge = jnp.zeros((16, 2, 8, C), F32)
    wide[:, :, 0:8, :] = edge
    wide[:, :, 40:48, :] = edge
    line = jnp.zeros((32, 3 * C), BF16)
    fan[0, 0] = line
    fan[16, 1] = line


def spread(wide, fan):
    for dx in range(3):
        lanes = slice(dx * C, (dx + 1) * C)
        columns = slice(LEFT - 1 + dx, LEFT + 31 + dx)
        fan[0:16, 1, :, lanes] = wide[:, 0, columns, :].astype(BF16)
        fan[1:17, 0, :, lanes] = wide[:, 1, columns, :].astype(BF16)


def row_window(fan, row, lanes=slice(0, 3 * C)):
    return fan[row // 2 : row // 2 + 16, row % 2, :, lanes].reshape(512, -1)


def convolve(fan, w):
    rows = jnp.concatenate([row_window(fan, row) for row in range(4)], axis=1)
    return jnp.dot(rows, paired_matrix(w), preferred_element_type=F32)


def paired_matrix(w):
    zero = jnp.zeros((C, C), BF16)
    columns = []
    for out in range(2):
        blocks = [
            w[3 * (row - out) + dx] if 0 <= row - out <= 2 else zero
            for row in range(4)
            for dx in range(3)
        ]
        columns.append(jnp.concatenate(blocks, axis=0))
    return jnp.concatenate(columns, axis=1)


def forward_layer(w, bias, wide, fan, slope=None):
    z = convolve(fan, w) + jnp.concatenate([bias, bias], axis=1)
    t = jnp.tanh(z)
    for half in range(2):
        part = t[:, half * C : (half + 1) * C].reshape(16, 32, C)
        wide[:, half, LEFT : LEFT + 32, :] += STEP_SIZE * part
        if slope is not None:
            slope[:, half] = STEP_SIZE * (1.0 - part * part)


def backward_layer(w, wide, fan, adjoint, slope):
    wide[:, :, LEFT : LEFT + 32, :] = adjoint[...] * slope[...]
    spread(wide, fan)
    back = convolve(fan, w)
    for half in range(2):
        adjoint[:, half] += back[:, half * C : (half + 1) * C].reshape(16, 32, C)


def first_kernel(length, state, w, bias, out, wide, fan, state_in, w_in, bias_in, sems):
    j = pl.program_id(0)
    load_state = pltpu.make_async_copy(state, state_in, sems.at[LMAX])
    load_bias = pltpu.make_async_copy(bias, bias_in, sems.at[LMAX + 1])

    def load_weights(slot):
        return pltpu.make_async_copy(w.at[slot], w_in.at[slot], sems.at[slot])

    @pl.when(j == 0)
    def _():
        load_state.start()
        load_weights(0).start()
        load_bias.start()
        clear_edges(wide, fan)
        load_state.wait()
        wide[:, :, LEFT : LEFT + 32, :] = state_in[...].astype(F32)
        load_bias.wait()

    for slot in range(LMAX):

        @pl.when(j == slot)
        def _():
            load_weights(slot).wait()
            if slot == 0:
                for later in range(1, LMAX):
                    load_weights(later).start()

    @pl.when(j < length[0])
    def _():
        spread(wide, fan)
        forward_layer(w_in.at[j], bias_in[pl.ds(j, 1), :], wide, fan)

    @pl.when(j == LMAX - 1)
    def _():
        out[...] = wide[:, :, LEFT : LEFT + 32, :].astype(BF16)


def prepare_kernel(length, w, ahead, behind):
    ahead[...] = w[...]
    for tap in range(TAPS):
        behind[0, tap] = w[0, TAPS - 1 - tap].T


def second_kernel(
    length, given, received, terminal, ahead, behind, bias, ending, back, states, slopes, wide, fan, kept, adjoint
):
    step = pl.program_id(0)
    leading = lax.axis_index("layer") == 0

    @pl.when(step == 0)
    def _():
        clear_edges(wide, fan)
        adjoint[...] = terminal[...].astype(F32)

    @pl.when(jnp.logical_and(step == 0, leading))
    def _():
        wide[:, :, LEFT : LEFT + 32, :] = given[...].astype(F32)

    @pl.when(jnp.logical_and(step == 0, jnp.logical_not(leading)))
    def _():
        wide[:, :, LEFT : LEFT + 32, :] = received[...].astype(F32)

    @pl.when(step < length[0])
    def _():
        spread(wide, fan)
        states[0, :, 0] = fan[0:16, 1, :, C : 2 * C]
        states[0, :, 1] = fan[1:17, 0, :, C : 2 * C]
        forward_layer(ahead.at[0], bias[pl.ds(step, 1), :], wide, fan, kept.at[step])
        slopes[0] = kept[step]

    @pl.when(step == LMAX - 1)
    def _():
        ending[...] = wide[:, :, LEFT : LEFT + 32, :].astype(BF16)

    slot = 2 * LMAX - 1 - step

    @pl.when(jnp.logical_and(step >= LMAX, slot < length[0]))
    def _():
        backward_layer(behind.at[0], wide, fan, adjoint, kept.at[slot])

    @pl.when(step == 2 * LMAX - 1)
    def _():
        back[...] = adjoint[...].astype(BF16)


def turn_kernel(length, states, turned, wide):
    j = pl.program_id(0)

    @pl.when(j == 0)
    def _():
        edge = jnp.zeros((16, 2, 8, C), F32)
        wide[:, :, 0:8, :] = edge
        wide[:, :, 40:48, :] = edge

    @pl.when(j < length[0])
    def _():
        wide[:, :, LEFT : LEFT + 32, :] = states[0].astype(F32)
        for dx in range(3):
            for half in range(2):
                part = wide[:, half, LEFT - 1 + dx : LEFT + 31 + dx, :].reshape(512, C)
                turned[0, dx * C : (dx + 1) * C, half * 512 : (half + 1) * 512] = part.astype(BF16).T


def gradient_layer(slot, length, w, turned, slope, wide, fan, adjoint, sums, total):
    @pl.when(slot < length[0])
    def _():
        backward_layer(w, wide, fan, adjoint, slope)
        middle = slice(C, 2 * C)
        signals = jnp.concatenate(
            [
                jnp.concatenate([row_window(fan, half + 2 - dy, middle) for dy in range(3)], axis=1)
                for half in range(2)
            ],
            axis=0,
        )
        total[...] = jnp.dot(turned, signals, preferred_element_type=F32)
        sums[pl.ds(slot, 1), :] = jnp.sum(
            signals[:, C : 2 * C].astype(F32), axis=0, keepdims=True
        )

    @pl.when(slot >= length[0])
    def _():
        total[...] = jnp.zeros_like(total)


def third_kernel(length, given, received, w, turned, slopes, adjoint, sums, *rest):
    messages, (wide, fan, total) = rest[:SIDE], rest[SIDE:]
    sample = lax.axis_index("sample")
    x, y = lax.rem(sample, SIDE), sample // SIDE
    step = pl.program_id(0)
    slot = LMAX - 1 - step
    trailing = lax.axis_index("layer") == lax.axis_size("layer") - 1

    @pl.when(step == 0)
    def _():
        clear_edges(wide, fan)
        sums[...] = jnp.zeros_like(sums)

    @pl.when(jnp.logical_and(step == 0, trailing))
    def _():
        adjoint[...] = given[...].astype(F32)

    @pl.when(jnp.logical_and(step == 0, jnp.logical_not(trailing)))
    def _():
        adjoint[...] = received[...].astype(F32)

    gradient_layer(
        slot, length, w.at[0], turned[0], slopes.at[0], wide, fan, adjoint, sums, total
    )
    base = (slot - HALF) * TAPS
    for right in range(SIDE):
        for down in range(SIDE):
            target = SIDE * lax.rem(y + down, SIDE) + lax.rem(x + right, SIDE)
            for dy in range(3):
                for dx in range(3):
                    rows = pl.ds(pl.multiple_of(dx * C + 8 * target, 8), 8)
                    block = total[rows, dy * C : (dy + 1) * C]
                    messages[right][down, base + 3 * dy + dx] = block.astype(BF16)


def merge_kernel(own, right, across, left, *outs):
    total = own[...].astype(F32) + right[...].astype(F32)
    total = total + across[...].astype(F32) + left[...].astype(F32)
    outs[0][...] = total[0]
    for down in range(1, SIDE):
        outs[down][...] = total[down].astype(BF16)


def fourth_kernel(
    length, adjoint_in, sums_in, w, turned, slopes, start, grads, wide, fan, adjoint, sums, total
):
    step = pl.program_id(0)
    slot = HALF - 1 - step

    @pl.when(step == 0)
    def _():
        clear_edges(wide, fan)
        sums[...] = sums_in[...]
        adjoint[...] = adjoint_in[...]

    gradient_layer(
        slot, length, w.at[0], turned[0], slopes.at[0], wide, fan, adjoint, sums, total
    )
    for dy in range(3):
        for dx in range(3):
            block = total[dx * C : (dx + 1) * C, dy * C : (dy + 1) * C]
            grads[:, slot * TAPS + 3 * dy + dx] = block.reshape(16, 8, C).astype(BF16)

    @pl.when(step == HALF - 1)
    def _():
        start[...] = adjoint[...].astype(BF16)
        for target in range(16):
            grads[target, HALF * TAPS] = pltpu.roll(sums[...], (C - 8 * target) % C, 1).astype(BF16)


def finish_kernel(factor, late, own, one, two, three, weight, bias):
    total = jnp.sum(late[...].astype(F32), axis=0) * factor
    weight[: HALF * TAPS] = total[: HALF * TAPS]
    bias[...] = total[HALF * TAPS, :LMAX, :8]
    early = own[...] + one[...].astype(F32) + two[...].astype(F32) + three[...].astype(F32)
    weight[HALF * TAPS :] = early * factor


IMAGE = (16, 2, 32, C)
WIDE = pltpu.VMEM((16, 2, 48, C), F32)
FAN = pltpu.VMEM((17, 2, 32, 3 * C), BF16)
CONV_FLOPS = 2 * 1024 * 9 * C * C


def whole(shape):
    return pl.BlockSpec(shape, lambda *_: (0,) * len(shape))


def slotted(shape, slot_of):
    rest = (0,) * len(shape)
    return pl.BlockSpec((1,) + shape, lambda step, *_: (slot_of(step),) + rest)


def call(kernel, steps, ins, outs, shapes, scratch, flops, vmem=14 * 2**20):
    return pl.pallas_call(
        kernel,
        out_shape=shapes,
        grid_spec=pltpu.PrefetchScalarGridSpec(
            num_scalar_prefetch=1, grid=(steps,), in_specs=ins, out_specs=outs, scratch_shapes=scratch
        ),
        compiler_params=pltpu.CompilerParams(
            dimension_semantics=("arbitrary",), vmem_limit_bytes=vmem
        ),
        cost_estimate=pl.CostEstimate(flops=flops, bytes_accessed=4 * 2**20, transcendentals=0),
    )


def body(section_lengths, forward_states, adjoint_states, weights, biases):
    given_state = forward_states.reshape(IMAGE)
    given_adjoint = adjoint_states.reshape(IMAGE)
    image = jax.ShapeDtypeStruct(IMAGE, BF16)
    taps = (TAPS, C, C)
    up = slotted(taps, lambda step: step)
    down = slotted(taps, lambda step: LMAX - 1 - step)

    hbm = pl.BlockSpec(memory_space=pltpu.HBM)
    propagated = call(
        first_kernel, LMAX,
        [hbm, hbm, hbm],
        whole(IMAGE), image,
        [
            WIDE, FAN, pltpu.VMEM(IMAGE, BF16), pltpu.VMEM((LMAX,) + taps, BF16),
            pltpu.VMEM((LMAX, C), F32), pltpu.SemaphoreType.DMA((LMAX + 2,)),
        ],
        LMAX * CONV_FLOPS, 63 * 2**20,
    )(section_lengths, given_state, weights, biases)
    received = shift_by(propagated, "layer", 1)

    weights_like = jax.ShapeDtypeStruct((LMAX,) + taps, BF16)
    ahead, behind = call(
        prepare_kernel, LMAX, [up], [up, up], [weights_like, weights_like], [], 10**6
    )(section_lengths, weights)

    ending, back_start, states, slopes = call(
        second_kernel, 2 * LMAX,
        [
            whole(IMAGE), whole(IMAGE), whole(IMAGE),
            slotted(taps, lambda step: jnp.minimum(step, LMAX - 1)),
            slotted(taps, lambda step: jnp.minimum(2 * LMAX - 1 - step, LMAX - 1)),
            whole((LMAX, C)),
        ],
        [
            whole(IMAGE), whole(IMAGE),
            slotted(IMAGE, lambda step: jnp.minimum(step, LMAX - 1)),
            slotted(IMAGE, lambda step: jnp.minimum(step, LMAX - 1)),
        ],
        [
            image, image,
            jax.ShapeDtypeStruct((LMAX,) + IMAGE, BF16),
            jax.ShapeDtypeStruct((LMAX,) + IMAGE, F32),
        ],
        [WIDE, FAN, pltpu.VMEM((LMAX,) + IMAGE, F32), pltpu.VMEM(IMAGE, F32)],
        2 * LMAX * CONV_FLOPS,
    )(section_lengths, given_state, received, given_adjoint, ahead, behind, biases)
    received_back = shift_by(back_start, "layer", -1)

    turned = call(
        turn_kernel, LMAX,
        [slotted(IMAGE, lambda step: step)],
        slotted((3 * C, 1024), lambda step: step),
        jax.ShapeDtypeStruct((LMAX, 3 * C, 1024), BF16),
        [WIDE], 10**6,
    )(section_lengths, states)

    middle = jax.ShapeDtypeStruct(IMAGE, F32)
    tally = jax.ShapeDtypeStruct((8, C), F32)
    message = (SIDE, HALF * TAPS, 8, C)
    total = pltpu.VMEM((3 * C, 3 * C), F32)
    adjoint, sums, *messages = call(
        third_kernel, HALF,
        [
            whole(IMAGE), whole(IMAGE), down,
            slotted((3 * C, 1024), lambda step: LMAX - 1 - step),
            slotted(IMAGE, lambda step: LMAX - 1 - step),
        ],
        [whole(IMAGE), whole((8, C))] + [whole(message)] * SIDE,
        [middle, tally] + [jax.ShapeDtypeStruct(message, BF16)] * SIDE,
        [WIDE, FAN, total],
        2 * HALF * CONV_FLOPS,
    )(section_lengths, given_adjoint, received_back, behind, turned, slopes)
    got = []
    for k in (1, 2, 3):
        got.append(send_ahead(messages[k], True, k))

    starting, grads = call(
        fourth_kernel, HALF,
        [
            whole(IMAGE), whole((8, C)),
            slotted(taps, lambda step: HALF - 1 - step),
            slotted((3 * C, 1024), lambda step: HALF - 1 - step),
            slotted(IMAGE, lambda step: HALF - 1 - step),
        ],
        [whole(IMAGE), whole((16, HALF * TAPS + 1, 8, C))],
        [image, jax.ShapeDtypeStruct((16, HALF * TAPS + 1, 8, C), BF16)],
        [WIDE, FAN, pltpu.VMEM(IMAGE, F32), pltpu.VMEM((8, C), F32), total],
        2 * HALF * CONV_FLOPS,
    )(section_lengths, adjoint, sums, behind, turned, slopes)
    late = lax.all_to_all(grads, "sample", 0, 0)

    piece = message[1:]
    merged = pl.pallas_call(
        merge_kernel,
        name="merge",
        out_shape=[jax.ShapeDtypeStruct(piece, F32)] + [jax.ShapeDtypeStruct(piece, BF16)] * 3,
        compiler_params=pltpu.CompilerParams(vmem_limit_bytes=16 * 2**20),
    )(messages[0], *got)
    early = [merged[0]] + [send_ahead(merged[k], False, k) for k in (1, 2, 3)]

    total_samples = forward_states.shape[1] * lax.axis_size("sample")
    factor = 1.0 / math.sqrt(total_samples * forward_states.shape[2] * forward_states.shape[3])
    weight_part, bias_part = pl.pallas_call(
        functools.partial(finish_kernel, factor),
        name="finish",
        out_shape=(
            jax.ShapeDtypeStruct((LMAX * TAPS, 8, C), F32),
            jax.ShapeDtypeStruct((LMAX, 8), F32),
        ),
        compiler_params=pltpu.CompilerParams(vmem_limit_bytes=16 * 2**20),
    )(late, *early)
    weight_part = weight_part.reshape(LMAX, TAPS, 8, C)
    shape = forward_states.shape
    return (ending.reshape(shape), starting.reshape(shape), weight_part, bias_part)


def solution(mesh):
    placed = (
        P("layer"),
        P("layer", "sample", None, None, None),
        P("layer", "sample", None, None, None),
        P("layer", None, None, None),
        P("layer", None),
    )
    return jax.shard_map(
        body,
        mesh=mesh,
        in_specs=placed,
        out_specs=(
            P("layer", "sample", None, None, None),
            P("layer", "sample", None, None, None),
            P("layer", None, "sample", None),
            P("layer", "sample"),
        ),
        check_vma=False,
    )
```

time: 62.2 us -> 61.3 us (0.986)
  the two profiles are of different devices: /device:TPU:97 before, /device:TPU:24 now
where the time goes in v2:
time: 61.3 us; the launch traced here: 61 us
  waiting for transfers between devices  26.4 us (43%)
  starting transfers between devices  18.7 us (31%)
  Pallas kernels  13.3 us (22%)
  between operations  1.33 us (2%)
  local copies, waits for them, and re-layouts  1.28 us (2%)
    ppermute x6, waiting for transfers between devices, send_ahead(): return lax.ppermute(block, 'sample', route)  15.4 us
    ppermute x2, waiting for transfers between devices, shift_by(): lax.ppermute(block, axis, [(i, (i + distance) % count) for i in range(cou...  11 us
    ppermute x6, starting transfers between devices, send_ahead(): return lax.ppermute(block, 'sample', route)  8.6 us
    all_to_all x1, starting transfers between devices, body(): late = lax.all_to_all(grads, 'sample', 0, 0)  7.17 us
    pallas_call x1, Pallas kernels, body(): call(second_kernel, 2 * LMAX, [whole(IMAGE), whole(IMAGE), whole(IMAGE),...  3.86 us
    pallas_call x1, Pallas kernels, body(): call(first_kernel, LMAX, [hbm, hbm, hbm], whole(IMAGE), image, [WIDE, FAN...  3.45 us
    pallas_call x1, Pallas kernels, body(): call(fourth_kernel, HALF, [whole(IMAGE), whole((8, C)), slotted(taps, lam...  3.31 us
    ppermute x2, starting transfers between devices, shift_by(): lax.ppermute(block, axis, [(i, (i + distance) % count) for i in range(cou...  2.91 us
  transfers between devices with their start and end apart: 9, of which 7 were waited for; matrix products, arithmetic and copies ran while one was open for 0% of the time, Pallas kernels for 2%

profile of v2, /device:TPU:24, one launch (start us, length us, event | category | flops | bytes accessed | tf_op | source)
XLA Modules:
  0.0 61.0 jit_solution(3322030175583268934)
XLA Ops:
  1.3 3.4 %shard_map.84 = bf16[16,2,32,128]{3,2,1,0:T(8,128)(2,1)} custom-call(s32[1]{0:T(128)S(6)} %copy.9.length, bf16[16,2,32,128]{3,2,1,0:T(8,128)(2,1)} %bitcast.7, bf16[4,9,128,128]{3,2,1,0:T(8,128)(2,1)} %w.3, f32[4,128]{1,0:T(4,128)} %bias.3), custom_call_target="tpu_custom_call" | custom-call | flops 1207959552 | bytes 4194304 | tf_op jit(solution)/shard_map/pallas_call | solution.py:335
  4.7 1.0 %collective-permute-start = (bf16[16,2,32,128]{3,2,1,0:T(8,128)(2,1)}, bf16[16,2,32,128]{3,2,1,0:T(8,128)(2,1)S(1)}, u32[]{:S(2)}, u32[]{:S(2)}) collective-permute-start(bf16[16,2,32,128]{3,2,1,0:T(8,128)(2,1)} %shard_map.84), channel_id=1, source_target_pairs={{0,16},{16,32},{32,48},{48,64},{64,80},{80,96},{96,112},{112,128},... | collective-permute-start | bytes 786440 | tf_op jit(solution)/shard_map/ppermute | solution.py:25
  5.8 0.0 copy-start
  5.8 1.3 %copy-done = bf16[4,9,128,128]{3,2,1,0:T(8,128)(2,1)S(1)} copy-done((bf16[4,9,128,128]{3,2,1,0:T(8,128)(2,1)S(1)}, bf16[4,9,128,128]{3,2,1,0:T(8,128)(2,1)}, u32[]{:S(2)}) %copy-start) | copy-done | bytes 1179672
  7.0 0.0 copy-start.1
  7.0 0.0 copy-start.2
  7.0 0.0 copy-start.3
  7.0 0.7 %shard_map.85 = (bf16[4,9,128,128]{3,2,1,0:T(8,128)(2,1)S(1)}, bf16[4,9,128,128]{3,2,1,0:T(8,128)(2,1)S(1)}) custom-call(s32[1]{0:T(128)S(6)} %copy.9.length, bf16[4,9,128,128]{3,2,1,0:T(8,128)(2,1)S(1)} %copy-done), custom_call_target="tpu_custom_call" | custom-call | flops 1000000 | bytes 4194304 | tf_op jit(solution)/shard_map/pallas_call | solution.py:348
  7.8 7.7 %collective-permute-done.received = bf16[16,2,32,128]{3,2,1,0:T(8,128)(2,1)S(1)} collective-permute-done((bf16[16,2,32,128]{3,2,1,0:T(8,128)(2,1)}, bf16[16,2,32,128]{3,2,1,0:T(8,128)(2,1)S(1)}, u32[]{:S(2)}, u32[]{:S(2)}) %collective-permute-start) | collective-permute-done | bytes 262176 | tf_op jit(solution)/shard_map/ppermute | solution.py:25
  15.5 0.0 copy-done.1
  15.5 0.0 copy-done.2
  15.5 0.0 copy-done.3
  15.5 3.9 %shard_map.86 = (bf16[16,2,32,128]{3,2,1,0:T(8,128)(2,1)}, bf16[16,2,32,128]{3,2,1,0:T(8,128)(2,1)S(1)}, bf16[4,16,2,32,128]{4,3,2,1,0:T(8,128)(2,1)S(1)}, f32[4,16,2,32,128]{4,3,2,1,0:T(8,128)S(1)}) custom-call(s32[1]{0:T(128)S(6)} %copy.9.length, bf16[16,2,32,128]{3,2,1,0:T(8,128)(2,1)S(1)} %bitcast.8, ...), custom_call_target="tpu_custom_call" | custom-call | flops 2415919104 | bytes 4194304 | tf_op jit(solution)/shard_map/pallas_call | solution.py:352
  19.4 1.9 %collective-permute-start.1 = (bf16[16,2,32,128]{3,2,1,0:T(8,128)(2,1)S(1)}, bf16[16,2,32,128]{3,2,1,0:T(8,128)(2,1)S(1)}, u32[]{:S(2)}, u32[]{:S(2)}) collective-permute-start(bf16[16,2,32,128]{3,2,1,0:T(8,128)(2,1)S(1)} %get-tuple-element.27), channel_id=1, source_target_pairs={{0,240},{16,0},{32,16},{48,32},{64,48},{80,64},{96,80},{112,96},{1... | collective-permute-start | bytes 786440 | tf_op jit(solution)/shard_map/ppermute | solution.py:25
  21.2 0.6 %shard_map.87.turned = bf16[4,384,1024]{2,1,0:T(8,128)(2,1)S(1)} custom-call(s32[1]{0:T(128)S(6)} %copy.9.length, bf16[4,16,2,32,128]{4,3,2,1,0:T(8,128)(2,1)S(1)} %get-tuple-element.28.states), custom_call_target="tpu_custom_call" | custom-call | flops 1000000 | bytes 4194304 | tf_op jit(solution)/shard_map/pallas_call | solution.py:375
  21.9 3.3 %collective-permute-done.1.received = bf16[16,2,32,128]{3,2,1,0:T(8,128)(2,1)S(1)} collective-permute-done((bf16[16,2,32,128]{3,2,1,0:T(8,128)(2,1)S(1)}, bf16[16,2,32,128]{3,2,1,0:T(8,128)(2,1)S(1)}, u32[]{:S(2)}, u32[]{:S(2)}) %collective-permute-start.1) | collective-permute-done | bytes 262176 | tf_op jit(solution)/shard_map/ppermute | solution.py:25
  25.1 0.5 shard_map.88
  25.6 3.3 %shard_map.89 = (bf16[16,2,32,128]{3,2,1,0:T(8,128)(2,1)}, bf16[16,19,8,128]{3,2,1,0:T(8,128)(2,1)}) custom-call(s32[1]{0:T(128)S(6)} %copy.9.length, f32[16,2,32,128]{3,2,1,0:T(8,128)S(1)} %get-tuple-element.30.adjoint_in, f32[8,128]{1,0:T(8,128)S(1)} %get-tuple-element.31.sums_in, bf16[4,9,128,128]{3,2,1,0:T(8,128)(2,1)S(1)} %get-tuple-element.25.behind.w, ...), custom_call_target="tpu_custom_call" | custom-call | flops 1207959552 | bytes 4194304 | tf_op jit(solution)/shard_map/pallas_call | solution.py:403
  28.9 7.2 %all-to-all-start = ((bf16[16,19,8,128]{3,2,1,0:T(8,128)(2,1)}), bf16[16,19,8,128]{3,2,1,0:T(8,128)(2,1)S(1)}, u32[]{:S(2)}, u32[]{:S(2)}) async-start(bf16[16,19,8,128]{3,2,1,0:T(8,128)(2,1)} %get-tuple-element.33), calls=%async_computation | async-start | bytes 1245184 | tf_op jit(solution)/shard_map/all_to_all | solution.py:416
  36.1 1.5 %collective-permute-start.2 = (bf16[4,18,8,128]{3,2,1,0:T(8,128)(2,1)S(1)}, bf16[4,18,8,128]{3,2,1,0:T(8,128)(2,1)S(1)}, u32[]{:S(2)}, u32[]{:S(2)}) collective-permute-start(bf16[4,18,8,128]{3,2,1,0:T(8,128)(2,1)S(1)} %get-tuple-element.35), channel_id=1, source_target_pairs={{0,1},{1,2},{2,3},{3,0},{4,5},{5,6},{6,7},{7,4},{8,9},{9,10},{10,1... | collective-permute-start | bytes 442376 | tf_op jit(solution)/shard_map/ppermute | solution.py:34
  37.6 2.7 %collective-permute-start.3 = (bf16[4,18,8,128]{3,2,1,0:T(8,128)(2,1)S(1)}, bf16[4,18,8,128]{3,2,1,0:T(8,128)(2,1)S(1)}, u32[]{:S(2)}, u32[]{:S(2)}) collective-permute-start(bf16[4,18,8,128]{3,2,1,0:T(8,128)(2,1)S(1)} %get-tuple-element.36), channel_id=1, source_target_pairs={{0,2},{1,3},{2,0},{3,1},{4,6},{5,7},{6,4},{7,5},{8,10},{9,11},{10,... | collective-permute-start | bytes 442376 | tf_op jit(solution)/shard_map/ppermute | solution.py:34
  40.2 1.5 %collective-permute-start.4 = (bf16[4,18,8,128]{3,2,1,0:T(8,128)(2,1)S(1)}, bf16[4,18,8,128]{3,2,1,0:T(8,128)(2,1)S(1)}, u32[]{:S(2)}, u32[]{:S(2)}) collective-permute-start(bf16[4,18,8,128]{3,2,1,0:T(8,128)(2,1)S(1)} %get-tuple-element.37), channel_id=1, source_target_pairs={{0,3},{1,0},{2,1},{3,2},{4,7},{5,4},{6,5},{7,6},{8,11},{9,8},{10,9... | collective-permute-start | bytes 442376 | tf_op jit(solution)/shard_map/ppermute | solution.py:34
  41.7 8.3 %collective-permute-done.2.right = bf16[4,18,8,128]{3,2,1,0:T(8,128)(2,1)S(1)} collective-permute-done((bf16[4,18,8,128]{3,2,1,0:T(8,128)(2,1)S(1)}, bf16[4,18,8,128]{3,2,1,0:T(8,128)(2,1)S(1)}, u32[]{:S(2)}, u32[]{:S(2)}) %collective-permute-start.2) | collective-permute-done | bytes 147488 | tf_op jit(solution)/shard_map/ppermute | solution.py:34
  50.0 2.0 %collective-permute-done.3.across = bf16[4,18,8,128]{3,2,1,0:T(8,128)(2,1)S(1)} collective-permute-done((bf16[4,18,8,128]{3,2,1,0:T(8,128)(2,1)S(1)}, bf16[4,18,8,128]{3,2,1,0:T(8,128)(2,1)S(1)}, u32[]{:S(2)}, u32[]{:S(2)}) %collective-permute-start.3) | collective-permute-done | bytes 147488 | tf_op jit(solution)/shard_map/ppermute | solution.py:34
  52.0 0.0 collective-permute-done.4.left
  52.0 0.1 merge.1
  52.1 0.6 %collective-permute-start.5 = (bf16[18,8,128]{2,1,0:T(8,128)(2,1)S(1)}, bf16[18,8,128]{2,1,0:T(8,128)(2,1)S(1)}, u32[]{:S(2)}, u32[]{:S(2)}) collective-permute-start(bf16[18,8,128]{2,1,0:T(8,128)(2,1)S(1)} %get-tuple-element.39), channel_id=1, source_target_pairs={{0,4},{1,5},{2,6},{3,7},{4,8},{5,9},{6,10},{7,11},{8,12},{9,13},{1... | collective-permute-start | bytes 110600 | tf_op jit(solution)/shard_map/ppermute | solution.py:34
  52.7 2.4 %collective-permute-start.6 = (bf16[18,8,128]{2,1,0:T(8,128)(2,1)S(1)}, bf16[18,8,128]{2,1,0:T(8,128)(2,1)S(1)}, u32[]{:S(2)}, u32[]{:S(2)}) collective-permute-start(bf16[18,8,128]{2,1,0:T(8,128)(2,1)S(1)} %get-tuple-element.40), channel_id=1, source_target_pairs={{0,8},{1,9},{2,10},{3,11},{4,12},{5,13},{6,14},{7,15},{8,0},{9,1},... | collective-permute-start | bytes 110600 | tf_op jit(solution)/shard_map/ppermute | solution.py:34
  55.1 0.0 collective-permute-start.7
  55.1 1.0 %collective-permute-done.5.one = bf16[18,8,128]{2,1,0:T(8,128)(2,1)S(1)} collective-permute-done((bf16[18,8,128]{2,1,0:T(8,128)(2,1)S(1)}, bf16[18,8,128]{2,1,0:T(8,128)(2,1)S(1)}, u32[]{:S(2)}, u32[]{:S(2)}) %collective-permute-start.5) | collective-permute-done | bytes 36896 | tf_op jit(solution)/shard_map/ppermute | solution.py:34
  56.1 2.1 %collective-permute-done.6.two = bf16[18,8,128]{2,1,0:T(8,128)(2,1)S(1)} collective-permute-done((bf16[18,8,128]{2,1,0:T(8,128)(2,1)S(1)}, bf16[18,8,128]{2,1,0:T(8,128)(2,1)S(1)}, u32[]{:S(2)}, u32[]{:S(2)}) %collective-permute-start.6) | collective-permute-done | bytes 36896 | tf_op jit(solution)/shard_map/ppermute | solution.py:34
  58.2 2.1 %collective-permute-done.7.three = bf16[18,8,128]{2,1,0:T(8,128)(2,1)S(1)} collective-permute-done((bf16[18,8,128]{2,1,0:T(8,128)(2,1)S(1)}, bf16[18,8,128]{2,1,0:T(8,128)(2,1)S(1)}, u32[]{:S(2)}, u32[]{:S(2)}) %collective-permute-start.7) | collective-permute-done | bytes 36896 | tf_op jit(solution)/shard_map/ppermute | solution.py:34
  60.2 0.0 all-to-all-done.late
  60.2 0.8 %finish.1 = (f32[36,8,128]{2,1,0:T(8,128)}, f32[4,8]{1,0:T(4,128)}) custom-call(bf16[16,19,8,128]{3,2,1,0:T(8,128)(2,1)S(1)} %all-to-all-done.late, f32[18,8,128]{2,1,0:T(8,128)S(1)} %get-tuple-element.38.own, bf16[18,8,128]{2,1,0:T(8,128)(2,1)S(1)} %collective-permute-done.5.one, bf16[18,8,128]{2,1,0:T(8,128)(2,1)S(1)} %collective-permute-done.6.two, ...), custom_call_target="tpu_custom_call" | custom-call | tf_op jit(solution)/shard_map/finish/pallas_call | solution.py:429
Async XLA Ops:
  4.7 10.8 %collective-permute-start = (bf16[16,2,32,128]{3,2,1,0:T(8,128)(2,1)}, bf16[16,2,32,128]{3,2,1,0:T(8,128)(2,1)S(1)}, u32[]{:S(2)}, u32[]{:S(2)}) collective-permute-start(bf16[16,2,32,128]{3,2,1,0:T(8,128)(2,1)} %shard_map.84), channel_id=1, source_target_pairs={{0,16},{16,32},{32,48},{48,64},{64,80},{80,96},{96,112},{112,128},... | collective-permute-start | bytes 786440 | tf_op jit(solution)/shard_map/ppermute | solution.py:25
  5.8 1.3 %copy-start = (bf16[4,9,128,128]{3,2,1,0:T(8,128)(2,1)S(1)}, bf16[4,9,128,128]{3,2,1,0:T(8,128)(2,1)}, u32[]{:S(2)}) copy-start(bf16[4,9,128,128]{3,2,1,0:T(8,128)(2,1)} %w.3) | copy-start | bytes 3538948
  7.0 8.5 %copy-start.1 = (bf16[1,1,32,32,128]{4,3,2,1,0:T(8,128)(2,1)S(1)}, bf16[1,1,32,32,128]{4,3,2,1,0:T(8,128)(2,1)}, u32[]{:S(2)}) copy-start(bf16[1,1,32,32,128]{4,3,2,1,0:T(8,128)(2,1)} %param.7) | copy-start | bytes 786436
  7.0 8.5 %copy-start.2 = (bf16[1,1,32,32,128]{4,3,2,1,0:T(8,128)(2,1)S(1)}, bf16[1,1,32,32,128]{4,3,2,1,0:T(8,128)(2,1)}, u32[]{:S(2)}) copy-start(bf16[1,1,32,32,128]{4,3,2,1,0:T(8,128)(2,1)} %param.6) | copy-start | bytes 786436
  7.0 8.5 %copy-start.3 = (f32[4,128]{1,0:T(4,128)S(1)}, f32[4,128]{1,0:T(4,128)}, u32[]{:S(2)}) copy-start(f32[4,128]{1,0:T(4,128)} %bias.3) | copy-start | bytes 6148
  19.4 5.8 %collective-permute-start.1 = (bf16[16,2,32,128]{3,2,1,0:T(8,128)(2,1)S(1)}, bf16[16,2,32,128]{3,2,1,0:T(8,128)(2,1)S(1)}, u32[]{:S(2)}, u32[]{:S(2)}) collective-permute-start(bf16[16,2,32,128]{3,2,1,0:T(8,128)(2,1)S(1)} %get-tuple-element.27), channel_id=1, source_target_pairs={{0,240},{16,0},{32,16},{48,32},{64,48},{80,64},{96,80},{112,96},{1... | collective-permute-start | bytes 786440 | tf_op jit(solution)/shard_map/ppermute | solution.py:25
  28.9 31.3 %all-to-all-start = ((bf16[16,19,8,128]{3,2,1,0:T(8,128)(2,1)}), bf16[16,19,8,128]{3,2,1,0:T(8,128)(2,1)S(1)}, u32[]{:S(2)}, u32[]{:S(2)}) async-start(bf16[16,19,8,128]{3,2,1,0:T(8,128)(2,1)} %get-tuple-element.33), calls=%async_computation | async-start | bytes 1245184 | tf_op jit(solution)/shard_map/all_to_all | solution.py:416
  36.1 13.9 %collective-permute-start.2 = (bf16[4,18,8,128]{3,2,1,0:T(8,128)(2,1)S(1)}, bf16[4,18,8,128]{3,2,1,0:T(8,128)(2,1)S(1)}, u32[]{:S(2)}, u32[]{:S(2)}) collective-permute-start(bf16[4,18,8,128]{3,2,1,0:T(8,128)(2,1)S(1)} %get-tuple-element.35), channel_id=1, source_target_pairs={{0,1},{1,2},{2,3},{3,0},{4,5},{5,6},{6,7},{7,4},{8,9},{9,10},{10,1... | collective-permute-start | bytes 442376 | tf_op jit(solution)/shard_map/ppermute | solution.py:34
  37.6 14.4 %collective-permute-start.3 = (bf16[4,18,8,128]{3,2,1,0:T(8,128)(2,1)S(1)}, bf16[4,18,8,128]{3,2,1,0:T(8,128)(2,1)S(1)}, u32[]{:S(2)}, u32[]{:S(2)}) collective-permute-start(bf16[4,18,8,128]{3,2,1,0:T(8,128)(2,1)S(1)} %get-tuple-element.36), channel_id=1, source_target_pairs={{0,2},{1,3},{2,0},{3,1},{4,6},{5,7},{6,4},{7,5},{8,10},{9,11},{10,... | collective-permute-start | bytes 442376 | tf_op jit(solution)/shard_map/ppermute | solution.py:34
  40.2 11.7 %collective-permute-start.4 = (bf16[4,18,8,128]{3,2,1,0:T(8,128)(2,1)S(1)}, bf16[4,18,8,128]{3,2,1,0:T(8,128)(2,1)S(1)}, u32[]{:S(2)}, u32[]{:S(2)}) collective-permute-start(bf16[4,18,8,128]{3,2,1,0:T(8,128)(2,1)S(1)} %get-tuple-element.37), channel_id=1, source_target_pairs={{0,3},{1,0},{2,1},{3,2},{4,7},{5,4},{6,5},{7,6},{8,11},{9,8},{10,9... | collective-permute-start | bytes 442376 | tf_op jit(solution)/shard_map/ppermute | solution.py:34
  52.1 4.0 %collective-permute-start.5 = (bf16[18,8,128]{2,1,0:T(8,128)(2,1)S(1)}, bf16[18,8,128]{2,1,0:T(8,128)(2,1)S(1)}, u32[]{:S(2)}, u32[]{:S(2)}) collective-permute-start(bf16[18,8,128]{2,1,0:T(8,128)(2,1)S(1)} %get-tuple-element.39), channel_id=1, source_target_pairs={{0,4},{1,5},{2,6},{3,7},{4,8},{5,9},{6,10},{7,11},{8,12},{9,13},{1... | collective-permute-start | bytes 110600 | tf_op jit(solution)/shard_map/ppermute | solution.py:34
  52.7 5.5 %collective-permute-start.6 = (bf16[18,8,128]{2,1,0:T(8,128)(2,1)S(1)}, bf16[18,8,128]{2,1,0:T(8,128)(2,1)S(1)}, u32[]{:S(2)}, u32[]{:S(2)}) collective-permute-start(bf16[18,8,128]{2,1,0:T(8,128)(2,1)S(1)} %get-tuple-element.40), channel_id=1, source_target_pairs={{0,8},{1,9},{2,10},{3,11},{4,12},{5,13},{6,14},{7,15},{8,0},{9,1},... | collective-permute-start | bytes 110600 | tf_op jit(solution)/shard_map/ppermute | solution.py:34
  55.1 5.2 %collective-permute-start.7 = (bf16[18,8,128]{2,1,0:T(8,128)(2,1)S(1)}, bf16[18,8,128]{2,1,0:T(8,128)(2,1)S(1)}, u32[]{:S(2)}, u32[]{:S(2)}) collective-permute-start(bf16[18,8,128]{2,1,0:T(8,128)(2,1)S(1)} %get-tuple-element.41), channel_id=1, source_target_pairs={{0,12},{1,13},{2,14},{3,15},{4,0},{5,1},{6,2},{7,3},{8,4},{9,5},{1... | collective-permute-start | bytes 110600 | tf_op jit(solution)/shard_map/ppermute | solution.py:34
